TPU v7x, 256 devices: a whole 4x4x8 slice. The times are simulated.
256 devices in a mesh: grp: 32 (over x, z_hi, y), ep: 8 (over z_lo, core).
Axes of the slice: x: 4, y: 4, z: 8 (z_hi: 2, z_lo: 4; z = z_hi * 4 + z_lo), core: 2. Of those that a mesh axis runs over, the one named last changes fastest.
Arguments:
- queries: bfloat16 [1024, 2304], P('grp'), may hold values from -36 to 36, as said below
- residual: bfloat16 [1024, 2304], P(('grp', 'ep')), may hold values from -20 to 20
- gain: bfloat16 [2304], replicated, may hold values from 0.5 to 1.5
- key_pages: bfloat16 [2048, 128, 2304], P(('grp', 'ep')), may hold values from -6 to 6
- value_pages: bfloat16 [2048, 128, 2304], P(('grp', 'ep')), may hold values from -6 to 6
- page_table: int32 [1024, 32], P('grp'), may hold values from -1 to 63, as said below
- lengths: int32 [1024], P('grp'), may hold values from 1 to 4096, as said below
- split_flag: int32 [1024], P('grp'), may hold values from 0 to 1, as said below
- routes: int32 [1024, 2], P(('grp', 'ep')), may hold values from 0 to 7, all different within a row; in each aligned block of 4 rows (0 to 3, 4 to 7, ...) at most 2 rows name the same one
- gates: bfloat16 [1024, 2], P(('grp', 'ep')), may hold values from 0.19921875 to 1
- w_gate: bfloat16 [8, 2304, 5760], P('ep', None, 'grp'), may hold values from -0.125 to 0.125
- w_up: bfloat16 [8, 2304, 5760], P('ep', None, 'grp'), may hold values from -0.125 to 0.125
- w_down: bfloat16 [8, 5760, 2304], P('ep', 'grp'), may hold values from -0.078125 to 0.078125
Outputs:
- update: bfloat16 [1024, 2304], P(('grp', 'ep'))
Inputs may be any that keep to these rules, and one draw needn't show every extreme that they name: `page_table`: entries j with j * 128 < lengths[r] are pages of the row's group; no page is named twice within a group; the other entries are -1. `lengths`: A split request's first half, in the even group of its pair, is always 32 * 128 tokens; other rows are no longer. `split_flag`: in every group exactly one row is 1, at the same slot in both groups of each pair 2i, 2i + 1. `routes`: within the rows of one device no expert is named more than 2 times. `queries`: the two rows of a split request hold the same query.
All inputs are finite; a program needn't handle non-finite values.
Results may differ from a plain program's by a relative error of at most 0.015.
Values may be sent and summed in bfloat16 or wider, within the bound.
No kernel may reach another device: no remote copies, remote signals or barrier semaphores. Data moves between devices by JAX's collectives and lax.ppermute only.
A program may use at most 192 MiB of HBM per device.

v0:
```python
import jax
import jax.numpy as jnp
from jax import lax
from jax.sharding import PartitionSpec as P

HEAD_DIM = 64
PAGE = 128
NEG_FILL = -1e30
NORM_EPS = 1e-06


def joined_2(array, axis, combine):
    everything = jax.tree.map(lambda part: lax.all_gather(part, axis), array)
    leading = jax.tree.map(lambda part: part[0], everything)

    def turn(k, so_far):
        return combine(so_far, jax.tree.map(lambda part: part[k], everything))

    return lax.fori_loop(1, lax.axis_size(axis), turn, leading)


def from_partner(array, axis, bit):
    return lax.ppermute(array, axis, [(i, i ^ 1 << bit) for i in range(lax.axis_size(axis))])


def merge_parts(first_part, second_part):
    maxima_a, totals_a, weighted_a = first_part
    maxima_b, totals_b, weighted_b = second_part
    highest = jnp.maximum(maxima_a, maxima_b)
    factor_a = jnp.exp(maxima_a - highest)
    factor_b = jnp.exp(maxima_b - highest)
    head_count = maxima_a.shape[-1]
    shaped = weighted_a.shape
    wide = shaped[:-1] + (head_count, shaped[-1] // head_count)
    weighted = (
        weighted_a.reshape(wide) * factor_a[..., None]
        + weighted_b.reshape(wide) * factor_b[..., None]
    )
    return (highest, totals_a * factor_a + totals_b * factor_b, weighted.reshape(shaped))


def page_partials(group_q, page_rows, row_lengths, key_rows, value_rows, first_page):
    page_count = key_rows.shape[0]
    slot_count = group_q.shape[0]
    head_count = group_q.shape[1] // HEAD_DIM
    page_ids = first_page + jnp.arange(page_count, dtype=jnp.int32)
    table_steps = jnp.arange(page_rows.shape[1], dtype=jnp.int32)
    live_step = (table_steps * PAGE)[None, :] < row_lengths[:, None]
    matches = (page_rows[:, :, None] == page_ids[None, None, :]) & live_step[:, :, None]
    owned_page = jnp.any(matches, axis=1)
    where_at = jnp.sum(jnp.where(matches, table_steps[None, :, None], 0), axis=1)
    offsets = jnp.arange(PAGE, dtype=jnp.int32)
    token_pos = where_at[:, :, None] * PAGE + offsets[None, None, :]
    visible = (owned_page[:, :, None] & (token_pos < row_lengths[:, None, None])).reshape(
        slot_count, page_count * PAGE
    )
    query_heads = group_q.reshape(slot_count, head_count, HEAD_DIM)
    key_heads = key_rows.reshape(page_count * PAGE, head_count, HEAD_DIM)
    value_heads = value_rows.reshape(page_count * PAGE, head_count, HEAD_DIM)
    scores = jnp.einsum(
        "shd,khd->hsk", query_heads, key_heads, preferred_element_type=jnp.float32
    ) * HEAD_DIM ** (-0.5)
    scores = jnp.where(visible[None], scores, NEG_FILL)
    maxima = jnp.max(scores, axis=2)
    exp_terms = jnp.where(visible[None], jnp.exp(scores - maxima[..., None]), 0.0)
    totals = jnp.sum(exp_terms, axis=2)
    weights = exp_terms.astype(jnp.bfloat16)
    weighted = jnp.einsum("hsk,khd->shd", weights, value_heads, preferred_element_type=jnp.float32)
    return (maxima.T, totals.T, weighted.reshape(slot_count, head_count * HEAD_DIM))


def on_device(
    queries,
    residual,
    gain,
    key_pages,
    value_pages,
    page_table,
    lengths,
    split_flag,
    routes,
    gates,
    w_gate,
    w_up,
    w_down,
):
    req_dev = residual.shape[0]
    ep_size = lax.axis_size("ep")
    my_ep = lax.axis_index("ep")
    first_page = my_ep * key_pages.shape[0]
    maxima, totals, weighted = page_partials(
        queries, page_table, lengths, key_pages, value_pages, first_page
    )
    row_start = my_ep * req_dev
    merged = joined_2((maxima, totals, weighted), "ep", merge_parts)
    maxima = lax.dynamic_slice_in_dim(merged[0], row_start, req_dev, 0)
    totals = lax.dynamic_slice_in_dim(merged[1], row_start, req_dev, 0)
    weighted = lax.dynamic_slice_in_dim(merged[2], row_start, req_dev, 0)
    own_split = (lax.dynamic_slice_in_dim(split_flag, row_start, req_dev, 0) == 1)[:, None]
    partner = from_partner((maxima, totals, weighted), "grp", 0)
    joined = merge_parts((maxima, totals, weighted), partner)
    totals = jnp.where(own_split, joined[1], totals)
    weighted = jnp.where(own_split, joined[2], weighted)
    head_count = totals.shape[1]
    attn = (
        (weighted.reshape(req_dev, head_count, -1) / totals[..., None])
        .reshape(req_dev, -1)
        .astype(jnp.bfloat16)
    )
    stream = residual.astype(jnp.float32) + attn.astype(jnp.float32)
    normed = (
        stream
        * lax.rsqrt(jnp.mean(stream * stream, axis=-1, keepdims=True) + NORM_EPS)
        * gain.astype(jnp.float32)
    ).astype(jnp.bfloat16)
    capacity = max(2, (2 * req_dev + ep_size - 1) // ep_size)
    slot_count = ep_size * capacity
    chosen = routes.reshape(-1)
    one_hot = (chosen[:, None] == jnp.arange(ep_size, dtype=jnp.int32)[None, :]).astype(jnp.int32)
    ranking = jnp.sum((jnp.cumsum(one_hot, axis=0) - one_hot) * one_hot, axis=1)
    slot_of = chosen * capacity + ranking
    slot_ids = jnp.arange(slot_count, dtype=jnp.int32)
    placing = (slot_ids[:, None] == slot_of[None, :]).astype(jnp.bfloat16)
    doubled = jnp.repeat(normed, 2, axis=0)
    outgoing = (
        jnp.dot(placing, doubled, preferred_element_type=jnp.float32)
        .astype(jnp.bfloat16)
        .reshape(ep_size, capacity, -1)
    )
    arrived = lax.all_to_all(outgoing, "ep", split_axis=0, concat_axis=0, tiled=True).reshape(
        slot_count, -1
    )
    gate_matrix = w_gate[0]
    up_matrix = w_up[0]
    down_matrix = w_down[0]
    block_rows = lax.all_gather(arrived, "grp", axis=0, tiled=True)
    gate_part = jnp.dot(block_rows, gate_matrix, preferred_element_type=jnp.float32)
    up_part = jnp.dot(block_rows, up_matrix, preferred_element_type=jnp.float32)
    inner = (jax.nn.silu(gate_part) * up_part).astype(jnp.bfloat16)
    block_rows = inner
    summed = lax.psum_scatter(
        jnp.dot(block_rows, down_matrix, preferred_element_type=jnp.float32).astype(jnp.bfloat16),
        "grp",
        scatter_dimension=0,
        tiled=True,
    )
    results = summed.reshape(ep_size, capacity, -1)
    returned = lax.all_to_all(results, "ep", split_axis=0, concat_axis=0, tiled=True)
    picking = (slot_of[:, None] == slot_ids[None, :]).astype(jnp.float32) * gates.reshape(-1)[
        :, None
    ].astype(jnp.float32)
    blending = picking.reshape(req_dev, 2, slot_count).sum(axis=1).astype(jnp.bfloat16)
    mixture = jnp.dot(
        blending, returned.reshape(slot_count, -1), preferred_element_type=jnp.float32
    )
    return (attn.astype(jnp.float32) + mixture).astype(jnp.bfloat16)


def solution(mesh):
    in_specs = (
        P("grp", None),
        P(("grp", "ep"), None),
        P(),
        P(("grp", "ep"), None, None),
        P(("grp", "ep"), None, None),
        P("grp", None),
        P("grp"),
        P("grp"),
        P(("grp", "ep"), None),
        P(("grp", "ep"), None),
        P("ep", None, "grp"),
        P("ep", None, "grp"),
        P("ep", "grp", None),
    )
    out_specs = P(("grp", "ep"), None)
    return jax.shard_map(
        on_device, mesh=mesh, in_specs=in_specs, out_specs=out_specs, check_vma=False
    )
```

profile of v0, /device:TPU:1, one launch (start us, length us, event | category | flops | bytes accessed | tf_op | source)
XLA Modules:
  0.0 495.6 jit_solution(9139386518411092309)
XLA Ops:
  7.4 1.4 select_reduce_fusion
  8.8 1.4 fusion.33
  10.2 7.1 %copy.64 = bf16[8,128,2304]{1,0,2:T(8,128)(2,1)} copy(bf16[8,128,2304]{2,1,0:T(8,128)(2,1)} %param.18) | data formatting | bytes 9437184 | tf_op args[3]
  17.3 8.2 %reshape.186 = bf16[1024,36,64]{0,2,1:T(8,128)(2,1)} reshape(bf16[8,128,2304]{1,0,2:T(8,128)(2,1)} %copy.64) | data formatting | bytes 9437184 | tf_op jit(solution)/shard_map/reshape | solution.py:58
  25.8 7.0 %copy.68 = bf16[8,128,2304]{1,0,2:T(8,128)(2,1)} copy(bf16[8,128,2304]{2,1,0:T(8,128)(2,1)} %param.19) | data formatting | bytes 9437184 | tf_op args[4]
  32.8 8.2 %reshape.187 = bf16[1024,36,64]{0,2,1:T(8,128)(2,1)} reshape(bf16[8,128,2304]{1,0,2:T(8,128)(2,1)} %copy.68) | data formatting | bytes 9437184 | tf_op jit(solution)/shard_map/reshape | solution.py:59
  41.3 3.6 fusion.3
  45.0 1.4 fusion.14
  47.4 0.9 all_gather_reshape.3
  48.4 3.7 fusion.6
  52.2 17.1 %all-gather.1 = f32[256,36]{1,0:T(8,128)S(1)} all-gather(f32[32,36]{1,0:T(8,128)S(1)} %copy.67), channel_id=3, replica_groups=mesh['grp'=32,'ep'=8] {'ep'}, dimensions={0}, use_global_device_ids=true | all-gather | bytes 41472 | tf_op jit(solution)/shard_map/all_gather | solution.py:13
  69.4 14.3 %all-gather = f32[256,36]{1,0:T(8,128)S(1)} all-gather(f32[32,36]{1,0:T(8,128)S(1)} %copy.66), channel_id=2, replica_groups=mesh['grp'=32,'ep'=8] {'ep'}, dimensions={0}, use_global_device_ids=true | all-gather | bytes 41472 | tf_op jit(solution)/shard_map/all_gather | solution.py:13
  84.2 7.2 %all-gather.5.cloned.1.call-done = f32[8,32,2304]{2,1,0:T(8,128)} async-done(((f32[1,32,2304]{2,1,0:T(8,128)}), f32[8,32,2304]{2,1,0:T(8,128)}) %all-gather.5.cloned.1.call-update) | async-done | bytes 2359312 | tf_op jit(solution)/shard_map/all_gather | solution.py:13
  91.4 1.0 slice_bitcast_fusion
  92.4 13.8 %while.19 = (s32[]{:T(128)}, f32[32,36]{1,0:T(8,128)S(1)}, f32[32,36]{1,0:T(8,128)S(1)}, f32[32,2304]{1,0:T(8,128)S(1)}, f32[8,32,36]{2,1,0:T(8,128)S(1)}, /*ind...) while((s32[]{:T(128)}, f32[32,36]{1,0:T(8,128)S(1)}, ...), condition=%wide.region_5.6_spmd, body=%wide.region_4.5_spmd.sunk | while | flops 228101 | bytes 3290263 | solution.py:19
  93.3 1.1 fusion.58
  95.3 1.1 fusion.58
  97.3 1.1 fusion.58
  99.3 1.1 fusion.58
  101.2 1.1 fusion.58
  103.2 1.1 fusion.58
  105.2 1.1 fusion.58
  106.9 1.0 collective-permute-start.2
  110.0 0.8 collective-permute-done.1
  111.3 11.3 %all_to_all.10 = bf16[8,2,2304]{2,1,0:T(2,128)(2,1)S(1)} all-to-all(bf16[8,2,2304]{2,1,0:T(2,128)(2,1)S(1)} %reshape.189), channel_id=1, replica_groups=mesh['grp'=32,'ep'=8] {'ep'}, dimensions={0} | all-to-all | bytes 147456 | tf_op jit(solution)/shard_map/all_to_all | solution.py:130
  123.4 89.5 %all-gather.7.cloned.1.call-done = bf16[512,2304]{1,0:T(8,128)(2,1)} async-done(((bf16[16,2304]{1,0:T(8,128)(2,1)}), bf16[512,2304]{1,0:T(8,128)(2,1)}) %all-gather.7.cloned.1.call-update) | async-done | bytes 2359312 | tf_op jit(solution)/shard_map/all_gather | solution.py:136
  212.9 2.8 fusion.21
  215.7 4.9 convolution_convert_fusion
  220.7 254.7 %reduce-scatter.2.cloned.1.call-done = bf16[16,2304]{1,0:T(8,128)(2,1)} async-done(((bf16[512,2304]{1,0:T(8,128)(2,1)}), bf16[16,2304]{1,0:T(8,128)(2,1)}) %reduce-scatter.2.cloned.1.call-update) | async-done | bytes 73744 | tf_op jit(solution)/shard_map/reduce_scatter | solution.py:141
  475.4 1.5 reshape.191
  476.9 6.2 %all-to-all-start.1 = ((bf16[8,2,2304]{2,1,0:T(2,128)(2,1)}), bf16[8,2,2304]{2,1,0:T(2,128)(2,1)S(1)}, u32[]{:S(2)}, u32[]{:S(2)}) async-start(bf16[8,2,2304]{2,1,0:T(2,128)(2,1)} %reshape.191), calls=%async_computation.2 | async-start | bytes 147456 | tf_op jit(solution)/shard_map/all_to_all | solution.py:148
  483.3 5.0 %all-to-all-done.1 = bf16[8,2,2304]{2,1,0:T(2,128)(2,1)S(1)} async-done(((bf16[8,2,2304]{2,1,0:T(2,128)(2,1)}), bf16[8,2,2304]{2,1,0:T(2,128)(2,1)S(1)}, u32[]{:S(2)}, u32[]{:S(2)}) %all-to-all-start.1) | async-done | bytes 73760 | tf_op jit(solution)/shard_map/all_to_all | solution.py:148
  (117 shorter events, 14.0 us)
Async XLA Ops:
  6.5 209.1 %copy-start = (bf16[1,180,2304]{2,1,0:T(8,128)(2,1)S(1)}, bf16[1,180,2304]{2,1,0:T(8,128)(2,1)}, u32[]{:S(2)}) copy-start(bf16[1,180,2304]{2,1,0:T(8,128)(2,1)} %param.27) | copy-start | bytes 2488324
  6.5 84.9 %all-gather.5.cloned.1.call-start = ((), (), s32[]{:S(2)}) async-start(), calls=%async_computation.3 | async-start | bytes 2654208 | tf_op jit(solution)/shard_map/all_gather | solution.py:13
  17.3 8.2 %copy-start.2 = (bf16[32,2304]{1,0:T(8,128)(2,1)S(1)}, bf16[32,2304]{1,0:T(8,128)(2,1)}, u32[]{:S(2)}) copy-start(bf16[32,2304]{1,0:T(8,128)(2,1)} %param.15) | copy-start | bytes 442372
  32.8 8.4 %copy-start.5 = (s32[32]{0:T(128)S(1)}, s32[32]{0:T(128)}, u32[]{:S(2)}) copy-start(s32[32]{0:T(128)} %param.21) | copy-start | bytes 388
  41.2 3.7 slice-start
  41.3 3.6 slice-start.1
  44.9 2.1 copy-start.1
  47.1 36.6 %copy-start.4 = (bf16[2304]{0:T(1024)(128)(2,1)S(1)}, bf16[2304]{0:T(1024)(128)(2,1)}, u32[]{:S(2)}) copy-start(bf16[2304]{0:T(1024)(128)(2,1)} %param.17) | copy-start | bytes 13828
  47.1 36.6 %copy-start.6 = (s32[4,2]{0,1:T(2,128)S(1)}, s32[4,2]{0,1:T(2,128)}, u32[]{:S(2)}) copy-start(s32[4,2]{0,1:T(2,128)} %param.23) | copy-start | bytes 100
  47.1 36.9 %copy-start.8 = (s32[32]{0:T(128)S(1)}, s32[32]{0:T(128)}, u32[]{:S(2)}) copy-start(s32[32]{0:T(128)} %param.22) | copy-start | bytes 388
  48.4 164.5 %all-gather.7.cloned.1.call-start = ((), (), s32[]{:S(2)}) async-start(), calls=%async_computation.4 | async-start | bytes 2433024 | tf_op jit(solution)/shard_map/all_gather | solution.py:136
  92.4 18.4 %copy-start.3 = (bf16[4,2304]{1,0:T(4,128)(2,1)S(1)}, bf16[4,2304]{1,0:T(4,128)(2,1)}, u32[]{:S(2)}) copy-start(bf16[4,2304]{1,0:T(4,128)(2,1)} %param.16) | copy-start | bytes 55300
  106.3 109.4 %copy-start.7 = (bf16[1,2304,180]{1,2,0:T(8,128)(2,1)S(1)}, bf16[1,2304,180]{1,2,0:T(8,128)(2,1)}, u32[]{:S(2)}) copy-start(bf16[1,2304,180]{1,2,0:T(8,128)(2,1)} %param.26) | copy-start | bytes 2488324
  106.3 2.5 collective-permute-start
  106.9 2.4 collective-permute-start.2
  107.9 2.9 collective-permute-start.1
  123.3 352.0 %reduce-scatter.2.cloned.1.call-start = ((), (), s32[]{:S(2)}) async-start(), calls=%async_computation.5 | async-start | bytes 2433024 | tf_op jit(solution)/shard_map/reduce_scatter | solution.py:141
  215.7 267.6 %copy-start.9 = (bf16[4,2]{0,1:T(2,128)(2,1)S(1)}, bf16[4,2]{0,1:T(2,128)(2,1)}, u32[]{:S(2)}) copy-start(bf16[4,2]{0,1:T(2,128)(2,1)} %param.24) | copy-start | bytes 52
  476.9 11.4 %all-to-all-start.1 = ((bf16[8,2,2304]{2,1,0:T(2,128)(2,1)}), bf16[8,2,2304]{2,1,0:T(2,128)(2,1)S(1)}, u32[]{:S(2)}, u32[]{:S(2)}) async-start(bf16[8,2,2304]{2,1,0:T(2,128)(2,1)} %reshape.191), calls=%async_computation.2 | async-start | bytes 147456 | tf_op jit(solution)/shard_map/all_to_all | solution.py:148
Sparse Core Ops, SparseCore 0:
  48.5 42.9 all-gather.4
  123.5 89.3 all-gather.6
  220.8 254.5 reduce-scatter.1
where the time goes:
time: 497 us; the launch traced here: 496 us
  waiting for transfers between devices  358 us (72%)
  local copies, waits for them, and re-layouts  43 us (9%)
  blocking collectives  42.7 us (9%)
  other arithmetic  16 us (3%)
  matrix products  13.6 us (3%)
  between operations  13.4 us (3%)
  starting transfers between devices  8.46 us (2%)
    reduce_scatter x1, waiting for transfers between devices, on_device(): lax.psum_scatter(jnp.dot(block_rows, down_matrix, preferred_element_type=...  255 us
    all_gather x1, waiting for transfers between devices, on_device(): block_rows = lax.all_gather(arrived, 'grp', axis=0, tiled=True)  89.5 us
    all_gather x2, blocking collectives, joined_2(): everything = jax.tree.map(lambda part: lax.all_gather(part, axis), array)  31.4 us
    unnamed x27, local copies, waits for them, and re-layouts  14.9 us
    all_to_all x1, blocking collectives, on_device(): lax.all_to_all(outgoing, 'ep', split_axis=0, concat_axis=0, tiled=True)  11.3 us
  transfers between devices with their start and end apart: 7, of which 7 were waited for; matrix products, arithmetic and copies ran while one was open for 1% of the time, Pallas kernels for 0%

commit v1 on v0

--- a/solution.py
+++ b/solution.py
@@ -84,6 +84,12 @@
     w_up,
     w_down,
 ):
+
+    def detail_column(xx):
+        return jnp.concatenate(
+            lax.all_to_all(jnp.stack([xx] * lax.axis_size("grp")), "grp", 0, 0), axis=0
+        )
+
     req_dev = residual.shape[0]
     ep_size = lax.axis_size("ep")
     my_ep = lax.axis_index("ep")
@@ -133,7 +139,7 @@
     gate_matrix = w_gate[0]
     up_matrix = w_up[0]
     down_matrix = w_down[0]
-    block_rows = lax.all_gather(arrived, "grp", axis=0, tiled=True)
+    block_rows = detail_column(arrived)
     gate_part = jnp.dot(block_rows, gate_matrix, preferred_element_type=jnp.float32)
     up_part = jnp.dot(block_rows, up_matrix, preferred_element_type=jnp.float32)
     inner = (jax.nn.silu(gate_part) * up_part).astype(jnp.bfloat16)

time: 497 us -> 471 us (0.948)
  waiting for transfers between devices: 358 us -> 271 us
  blocking collectives: 42.7 us -> 106 us
    all_gather x1 -> x0, waiting for transfers between devices: 89.5 us -> none  [on_device(): block_rows = lax.all_gather(arrived, 'grp', axis=0, tiled=True)]
    all_to_all x0 -> x1, blocking collectives: none -> 62.9 us  [detail_column(): lax.all_to_all(jnp.stack([xx] * lax.axis_size('grp')), 'grp', 0, 0)]
  transfers between devices with their start and end apart: 7 -> 6, of which waited for: 7 -> 6; matrix products, arithmetic and copies ran while one was open for 1% -> 1% of each run, Pallas kernels for 0% -> 0%
where the time goes in v1:
time: 471 us; the launch traced here: 470 us
  waiting for transfers between devices  271 us (58%)
  blocking collectives  106 us (23%)
  local copies, waits for them, and re-layouts  42.5 us (9%)
  other arithmetic  16 us (3%)
  between operations  13.7 us (3%)
  matrix products  12.1 us (3%)
  starting transfers between devices  8.38 us (2%)
    reduce_scatter x1, waiting for transfers between devices, on_device(): lax.psum_scatter(jnp.dot(block_rows, down_matrix, preferred_element_type=...  257 us
    all_to_all x1, blocking collectives, detail_column(): lax.all_to_all(jnp.stack([xx] * lax.axis_size('grp')), 'grp', 0, 0)  62.9 us
    all_gather x2, blocking collectives, joined_2(): everything = jax.tree.map(lambda part: lax.all_gather(part, axis), array)  31.4 us
    unnamed x27, local copies, waits for them, and re-layouts  14.9 us
    all_to_all x1, blocking collectives, on_device(): lax.all_to_all(outgoing, 'ep', split_axis=0, concat_axis=0, tiled=True)  11.3 us
  transfers between devices with their start and end apart: 6, of which 6 were waited for; matrix products, arithmetic and copies ran while one was open for 1% of the time, Pallas kernels for 0%

profile of v1, /device:TPU:1, one launch (start us, length us, event | category | flops | bytes accessed | tf_op | source)
XLA Modules:
  0.0 470.1 jit_solution(114311291496405839)
XLA Ops:
  7.4 1.4 select_reduce_fusion
  8.8 1.4 fusion.33
  10.2 7.1 %copy.64 = bf16[8,128,2304]{1,0,2:T(8,128)(2,1)} copy(bf16[8,128,2304]{2,1,0:T(8,128)(2,1)} %param.18) | data formatting | bytes 9437184 | tf_op args[3]
  17.3 8.2 %reshape.188 = bf16[1024,36,64]{0,2,1:T(8,128)(2,1)} reshape(bf16[8,128,2304]{1,0,2:T(8,128)(2,1)} %copy.64) | data formatting | bytes 9437184 | tf_op jit(solution)/shard_map/reshape | solution.py:58
  25.7 7.0 %copy.68 = bf16[8,128,2304]{1,0,2:T(8,128)(2,1)} copy(bf16[8,128,2304]{2,1,0:T(8,128)(2,1)} %param.19) | data formatting | bytes 9437184 | tf_op args[4]
  32.7 8.2 %reshape.189 = bf16[1024,36,64]{0,2,1:T(8,128)(2,1)} reshape(bf16[8,128,2304]{1,0,2:T(8,128)(2,1)} %copy.68) | data formatting | bytes 9437184 | tf_op jit(solution)/shard_map/reshape | solution.py:59
  41.3 3.6 fusion.3
  45.0 1.4 fusion.14
  47.4 0.9 all_gather_reshape.3
  48.4 3.7 fusion.6
  52.1 17.1 %all-gather.1 = f32[256,36]{1,0:T(8,128)S(1)} all-gather(f32[32,36]{1,0:T(8,128)S(1)} %copy.67), channel_id=3, replica_groups=mesh['grp'=32,'ep'=8] {'ep'}, dimensions={0}, use_global_device_ids=true | all-gather | bytes 41472 | tf_op jit(solution)/shard_map/all_gather | solution.py:13
  69.3 14.3 %all-gather = f32[256,36]{1,0:T(8,128)S(1)} all-gather(f32[32,36]{1,0:T(8,128)S(1)} %copy.66), channel_id=2, replica_groups=mesh['grp'=32,'ep'=8] {'ep'}, dimensions={0}, use_global_device_ids=true | all-gather | bytes 41472 | tf_op jit(solution)/shard_map/all_gather | solution.py:13
  84.2 7.2 %all-gather.4.cloned.1.call-done = f32[8,32,2304]{2,1,0:T(8,128)} async-done(((f32[1,32,2304]{2,1,0:T(8,128)}), f32[8,32,2304]{2,1,0:T(8,128)}) %all-gather.4.cloned.1.call-update) | async-done | bytes 2359312 | tf_op jit(solution)/shard_map/all_gather | solution.py:13
  91.4 1.0 slice_bitcast_fusion
  92.4 13.8 %while.19 = (s32[]{:T(128)}, f32[32,36]{1,0:T(8,128)S(1)}, f32[32,36]{1,0:T(8,128)S(1)}, f32[32,2304]{1,0:T(8,128)S(1)}, f32[8,32,36]{2,1,0:T(8,128)S(1)}, /*ind...) while((s32[]{:T(128)}, f32[32,36]{1,0:T(8,128)S(1)}, ...), condition=%wide.region_5.6_spmd, body=%wide.region_4.5_spmd.sunk | while | flops 228101 | bytes 3290263 | solution.py:19
  93.3 1.1 fusion.58
  95.3 1.1 fusion.58
  97.3 1.1 fusion.58
  99.2 1.1 fusion.58
  101.2 1.1 fusion.58
  103.2 1.1 fusion.58
  105.2 1.1 fusion.58
  106.9 1.0 collective-permute-start.2
  109.9 0.8 collective-permute-done.1
  111.3 11.3 %all_to_all.15 = bf16[8,2,2304]{2,1,0:T(2,128)(2,1)S(1)} all-to-all(bf16[8,2,2304]{2,1,0:T(2,128)(2,1)S(1)} %reshape.191), channel_id=1, replica_groups=mesh['grp'=32,'ep'=8] {'ep'}, dimensions={0} | all-to-all | bytes 147456 | tf_op jit(solution)/shard_map/all_to_all | solution.py:136
  122.8 62.9 %all_to_all.16 = bf16[32,16,2304]{2,1,0:T(8,128)(2,1)S(1)} all-to-all(bf16[32,16,2304]{2,1,0:T(8,128)(2,1)S(1)} %stack.3), channel_id=1, replica_groups=mesh['grp'=32,'ep'=8] {'grp'}, dimensions={0} | all-to-all | bytes 4718592 | tf_op jit(solution)/shard_map/all_to_all | solution.py:90
  185.8 1.7 fusion.21
  187.4 4.5 convolution_convert_fusion
  192.1 257.5 %reduce-scatter.2.cloned.1.call-done = bf16[16,2304]{1,0:T(8,128)(2,1)} async-done(((bf16[512,2304]{1,0:T(8,128)(2,1)}), bf16[16,2304]{1,0:T(8,128)(2,1)}) %reduce-scatter.2.cloned.1.call-update) | async-done | bytes 73744 | tf_op jit(solution)/shard_map/reduce_scatter | solution.py:147
  449.5 1.5 reshape.193
  451.1 6.2 %all-to-all-start.2 = ((bf16[8,2,2304]{2,1,0:T(2,128)(2,1)}), bf16[8,2,2304]{2,1,0:T(2,128)(2,1)S(1)}, u32[]{:S(2)}, u32[]{:S(2)}) async-start(bf16[8,2,2304]{2,1,0:T(2,128)(2,1)} %reshape.193), calls=%async_computation.3 | async-start | bytes 147456 | tf_op jit(solution)/shard_map/all_to_all | solution.py:154
  457.5 5.0 %all-to-all-done.2 = bf16[8,2,2304]{2,1,0:T(2,128)(2,1)S(1)} async-done(((bf16[8,2,2304]{2,1,0:T(2,128)(2,1)}), bf16[8,2,2304]{2,1,0:T(2,128)(2,1)S(1)}, u32[]{:S(2)}, u32[]{:S(2)}) %all-to-all-start.2) | async-done | bytes 73760 | tf_op jit(solution)/shard_map/all_to_all | solution.py:154
  (116 shorter events, 13.4 us)
Async XLA Ops:
  6.5 180.9 %copy-start = (bf16[1,180,2304]{2,1,0:T(8,128)(2,1)S(1)}, bf16[1,180,2304]{2,1,0:T(8,128)(2,1)}, u32[]{:S(2)}) copy-start(bf16[1,180,2304]{2,1,0:T(8,128)(2,1)} %param.27) | copy-start | bytes 2488324
  6.5 84.9 %all-gather.4.cloned.1.call-start = ((), (), s32[]{:S(2)}) async-start(), calls=%async_computation.4 | async-start | bytes 2654208 | tf_op jit(solution)/shard_map/all_gather | solution.py:13
  17.3 8.2 %copy-start.2 = (bf16[32,2304]{1,0:T(8,128)(2,1)S(1)}, bf16[32,2304]{1,0:T(8,128)(2,1)}, u32[]{:S(2)}) copy-start(bf16[32,2304]{1,0:T(8,128)(2,1)} %param.15) | copy-start | bytes 442372
  32.7 8.4 %copy-start.5 = (s32[32]{0:T(128)S(1)}, s32[32]{0:T(128)}, u32[]{:S(2)}) copy-start(s32[32]{0:T(128)} %param.21) | copy-start | bytes 388
  41.2 3.7 slice-start
  41.3 3.6 slice-start.1
  44.9 2.1 copy-start.1
  47.1 36.6 %copy-start.4 = (bf16[2304]{0:T(1024)(128)(2,1)S(1)}, bf16[2304]{0:T(1024)(128)(2,1)}, u32[]{:S(2)}) copy-start(bf16[2304]{0:T(1024)(128)(2,1)} %param.17) | copy-start | bytes 13828
  47.1 36.6 %copy-start.6 = (s32[4,2]{0,1:T(2,128)S(1)}, s32[4,2]{0,1:T(2,128)}, u32[]{:S(2)}) copy-start(s32[4,2]{0,1:T(2,128)} %param.23) | copy-start | bytes 100
  47.1 36.8 %copy-start.8 = (s32[32]{0:T(128)S(1)}, s32[32]{0:T(128)}, u32[]{:S(2)}) copy-start(s32[32]{0:T(128)} %param.22) | copy-start | bytes 388
  48.3 401.2 %reduce-scatter.2.cloned.1.call-start = ((), (), s32[]{:S(2)}) async-start(), calls=%async_computation.5 | async-start | bytes 2433024 | tf_op jit(solution)/shard_map/reduce_scatter | solution.py:147
  92.4 18.4 %copy-start.3 = (bf16[4,2304]{1,0:T(4,128)(2,1)S(1)}, bf16[4,2304]{1,0:T(4,128)(2,1)}, u32[]{:S(2)}) copy-start(bf16[4,2304]{1,0:T(4,128)(2,1)} %param.16) | copy-start | bytes 55300
  106.3 2.5 collective-permute-start
  106.9 2.4 collective-permute-start.2
  107.9 2.9 collective-permute-start.1
  122.7 63.1 %copy-start.7 = (bf16[1,2304,180]{1,2,0:T(8,128)(2,1)S(1)}, bf16[1,2304,180]{1,2,0:T(8,128)(2,1)}, u32[]{:S(2)}) copy-start(bf16[1,2304,180]{1,2,0:T(8,128)(2,1)} %param.25) | copy-start | bytes 2488324
  187.4 270.0 %copy-start.9 = (bf16[4,2]{0,1:T(2,128)(2,1)S(1)}, bf16[4,2]{0,1:T(2,128)(2,1)}, u32[]{:S(2)}) copy-start(bf16[4,2]{0,1:T(2,128)(2,1)} %param.24) | copy-start | bytes 52
  451.1 11.4 %all-to-all-start.2 = ((bf16[8,2,2304]{2,1,0:T(2,128)(2,1)}), bf16[8,2,2304]{2,1,0:T(2,128)(2,1)S(1)}, u32[]{:S(2)}, u32[]{:S(2)}) async-start(bf16[8,2,2304]{2,1,0:T(2,128)(2,1)} %reshape.193), calls=%async_computation.3 | async-start | bytes 147456 | tf_op jit(solution)/shard_map/all_to_all | solution.py:154
Sparse Core Ops, SparseCore 0:
  48.5 42.9 all-gather.3
  192.1 257.4 reduce-scatter.1
